TPU v7x, 32 devices: a whole 2x2x4 slice. The times are simulated.
32 devices in a mesh: hi: 4 (over z), mid: 4 (over x, core), lo: 2 (over y).
Axes of the slice: x: 2, y: 2, z: 4, core: 2. Of those that a mesh axis runs over, the one named last changes fastest.
Arguments:
- amplitudes: bfloat16 [1024, 16384], P('lo', ('hi', 'mid')), may hold values from -6 to 6
- hop_blocks: bfloat16 [4, 512, 512], replicated, may hold values from -1 to 2, as said below
- coupling_seed: int32 [14], replicated, may hold values from 1 to 7
Outputs:
- new_state: bfloat16 [1024, 16384], P('lo', ('hi', 'mid'))
Inputs may be any that keep to these rules, and one draw needn't show every extreme that they name: hop_blocks[k, a, b] is zero where a and b differ in their number of set bits.
All inputs are finite; a program needn't handle non-finite values.
Results may differ from a plain program's by a relative error of at most 0.0064.
Values may be sent and summed in bfloat16 or wider, within the bound.
A program may use at most 64 MiB of HBM per device.

v0:
```python
import jax
import jax.numpy as jnp
from jax import lax
from jax.sharding import PartitionSpec as P

BLOCK = 512
SITES = 14
COUPLING = 0.06


def occupancy(indices):
    site_ids = jnp.arange(SITES, dtype=jnp.int32)
    return (indices[:, None] >> site_ids[None, :] & 1).astype(jnp.float32)


def diagonal_factor(up_index, down_index, coupling_seed):
    up_occupied = occupancy(up_index)
    down_occupied = occupancy(down_index)
    strength = COUPLING * coupling_seed.astype(jnp.float32)
    energy = jnp.dot(
        up_occupied * strength[None, :], down_occupied.T, precision=lax.Precision.HIGHEST
    )
    return jnp.exp(-energy)


def on_device(amplitudes, hop_blocks, coupling_seed):
    down_rows, up_cols = amplitudes.shape
    groups = lax.axis_size(("hi", "mid"))
    lo_count = lax.axis_size("lo")
    split_view = amplitudes.reshape(down_rows, up_cols // BLOCK, BLOCK)
    first_pass = jnp.einsum(
        "dav,wv->awd", split_view, hop_blocks[0], preferred_element_type=jnp.float32
    ).astype(jnp.bfloat16)
    local_top = BLOCK // groups
    remainder = up_cols // local_top
    first_pass = first_pass.reshape(local_top, remainder, down_rows)
    moved = lax.all_to_all(first_pass, ("hi", "mid"), split_axis=1, concat_axis=0, tiled=True)
    second_pass = jnp.einsum(
        "gh,hpd->gpd", hop_blocks[1], moved, preferred_element_type=jnp.float32
    )
    span_low = remainder // groups
    up_index = (
        jnp.arange(BLOCK, dtype=jnp.int32)[:, None] * remainder
        + lax.axis_index(("hi", "mid")) * span_low
        + jnp.arange(span_low, dtype=jnp.int32)[None, :]
    ).reshape(-1)
    down_index = lax.axis_index("lo") * down_rows + jnp.arange(down_rows, dtype=jnp.int32)
    factor = diagonal_factor(up_index, down_index, coupling_seed).reshape(
        BLOCK, span_low, down_rows
    )
    mixed_pass = (second_pass * factor).astype(jnp.bfloat16)
    returned = lax.all_to_all(
        mixed_pass, ("hi", "mid"), split_axis=0, concat_axis=1, tiled=True
    ).reshape(up_cols, down_rows)
    third_pass = jnp.einsum(
        "ud,ed->eu", returned, hop_blocks[2], preferred_element_type=jnp.float32
    ).astype(jnp.bfloat16)
    gathered = lax.all_to_all(
        third_pass.reshape(BLOCK // lo_count, lo_count, up_cols),
        "lo",
        split_axis=1,
        concat_axis=0,
        tiled=True,
    )
    fourth_pass = jnp.einsum(
        "gh,hpu->gpu", hop_blocks[3], gathered, preferred_element_type=jnp.float32
    ).astype(jnp.bfloat16)
    result = lax.all_to_all(fourth_pass, "lo", split_axis=0, concat_axis=1, tiled=True).reshape(
        down_rows, up_cols
    )
    return result


def solution(mesh):
    in_specs = (P("lo", ("hi", "mid")), P(), P())
    out_specs = P("lo", ("hi", "mid"))
    return jax.shard_map(
        on_device, mesh=mesh, in_specs=in_specs, out_specs=out_specs, check_vma=False
    )
```

profile of v0, /device:TPU:0, one launch (start us, length us, event | category | flops | bytes accessed | tf_op | source)
XLA Modules:
  0.0 115.0 jit_solution(5764832066527705775)
XLA Ops:
  0.0 2.1 %convolution_convert_fusion.2 = bf16[512,512,2]{1,0,2:T(8,128)(2,1)S(1)} fusion(bf16[64,2,8,512]{3,2,1,0:T(8,128)(2,1)} %bitcast.57, bf16[4,512,512]{2,1,0:T(8,128)(2,1)} %param.4), kind=kOutput, calls=%fused_computation.5 | convolution fusion | flops 537395200 | bytes 2621440 | tf_op jit(solution)/shard_map/dav,wv->awd/dot_general | solution.py:31
  2.1 0.0 copy-start
  2.1 1.5 %copy.56 = bf16[32,32,512]{2,0,1:T(8,128)(2,1)} copy(bf16[32,32,512]{2,1,0:T(8,128)(2,1)S(1)} %bitcast.56) | data formatting | bytes 2097152 | tf_op jit(solution)/shard_map/reshape | solution.py:36
  3.7 7.4 %all-to-all-start = ((bf16[32,32,512]{2,0,1:T(8,128)(2,1)}), bf16[32,32,512]{2,0,1:T(8,128)(2,1)S(1)}, u32[]{:S(2)}, u32[]{:S(2)}) async-start(bf16[32,32,512]{2,0,1:T(8,128)(2,1)} %copy.56), calls=%async_computation | async-start | bytes 2097152 | tf_op jit(solution)/shard_map/all_to_all | solution.py:37
  11.1 0.1 iota_add_fusion
  11.2 0.2 add.50
  11.4 0.0 copy-done
  11.5 2.0 %negate_exponential_fusion = f32[1024,512]{1,0:T(8,128)S(1)} fusion(s32[512]{0:T(512)S(1)} %iota_add_fusion.1, f32[14]{0:T(128)S(1)} %convert_multiply_fusion, s32[1024]{0:T(1024)S(1)} %add.50), kind=kOutput, calls=%fused_computation.2 | convolution fusion | flops 88683520 | bytes 2103352 | tf_op jit(solution)/shard_map/dot_general | solution.py:20
  13.4 2.3 %reshape.54 = f32[512,2,512]{2,1,0:T(2,128)} reshape(f32[1024,512]{1,0:T(8,128)S(1)} %negate_exponential_fusion) | data formatting | bytes 4194304 | tf_op jit(solution)/shard_map/reshape | solution.py:48
  15.7 2.7 %copy.59 = f32[512,2,512]{0,2,1:T(8,128)S(1)} copy(f32[512,2,512]{2,1,0:T(2,128)} %reshape.54) | data formatting | bytes 4194304 | tf_op jit(solution)/shard_map/reshape | solution.py:48
  18.5 15.5 %all-to-all-done = bf16[32,32,512]{2,0,1:T(8,128)(2,1)S(1)} async-done(((bf16[32,32,512]{2,0,1:T(8,128)(2,1)}), bf16[32,32,512]{2,0,1:T(8,128)(2,1)S(1)}, u32[]{:S(2)}, u32[]{:S(2)}) %all-to-all-start) | async-done | bytes 1048608 | tf_op jit(solution)/shard_map/all_to_all | solution.py:37
  34.0 0.1 copy.57
  34.1 1.8 %fusion = bf16[512,2,512]{0,2,1:T(8,128)(2,1)S(1)} fusion(f32[512,2,512]{0,2,1:T(8,128)S(1)} %copy.59, bf16[512,2,512]{2,0,1:T(8,128)(2,1)S(1)} %bitcast.54, bf16[4,512,512]{2,1,0:T(8,128)(2,1)} %param.4), kind=kOutput, calls=%fused_computation.1 | convolution fusion | flops 537919488 | bytes 4718592 | tf_op jit(solution)/shard_map/gh,hpd->gpd/dot_general | solution.py:38
  35.9 1.0 copy.60
  36.9 31.3 %all_to_all.63 = bf16[512,2,512]{2,1,0:T(2,128)(2,1)S(1)} all-to-all(bf16[512,2,512]{2,1,0:T(2,128)(2,1)S(1)} %copy.60), channel_id=1, replica_groups=mesh['hi'=4,'mid'=4,'lo'=2] {'hi','mid'}, dimensions={0} | all-to-all | bytes 2097152 | tf_op jit(solution)/shard_map/all_to_all | solution.py:52
  68.1 0.2 copy.61
  68.3 1.1 copy.62
  69.4 0.4 reshape.55
  69.8 1.8 %fusion.1 = bf16[512,1024]{1,0:T(8,128)(2,1)S(1)} fusion(bf16[1024,512]{1,0:T(8,128)(2,1)S(1)} %reshape.55, bf16[4,512,512]{2,1,0:T(8,128)(2,1)} %param.4), kind=kOutput, calls=%fused_computation.6 | convolution fusion | flops 537395200 | bytes 2621440 | tf_op jit(solution)/shard_map/ud,ed->eu/dot_general | solution.py:55
  71.6 0.4 reshape.56
  72.1 0.3 copy.63
  72.4 17.5 %all_to_all.64 = bf16[256,2,1024]{2,0,1:T(8,128)(2,1)S(1)} all-to-all(bf16[256,2,1024]{2,0,1:T(8,128)(2,1)S(1)} %copy.63), channel_id=1, replica_groups=mesh['hi'=4,'mid'=4,'lo'=2] {'lo'}, dimensions={1} | all-to-all | bytes 2097152 | tf_op jit(solution)/shard_map/all_to_all | solution.py:58
  89.8 1.8 %fusion.2 = bf16[512,1,1024]{0,2,1:T(8,128)(2,1)S(1)} fusion(bf16[512,1024]{1,0:T(8,128)(2,1)S(1)} %bitcast.55, bf16[4,512,512]{2,1,0:T(8,128)(2,1)} %param.4), kind=kOutput, calls=%fused_computation.7 | convolution fusion | flops 537395200 | bytes 2621440 | tf_op jit(solution)/shard_map/gh,hpu->gpu/dot_general | solution.py:65
  91.6 0.5 broadcast.24
  92.1 1.5 %reduce = bf16[512,1024]{0,1:T(8,128)(2,1)S(1)} reduce(bf16[512,1,1024]{0,2,1:T(8,128)(2,1)S(1)} %fusion.2, bf16[]{:T(256)} %broadcast.24), dimensions={1}, to_apply=%copy.64.reduce_sub_computation | reduce | bytes 2097154 | tf_op jit(solution)/shard_map/convert_element_type | solution.py:67
  93.6 0.5 copy.73
  94.1 0.8 reshape.61
  94.9 16.5 %all_to_all.65 = bf16[2,2,131072]{2,1,0:T(2,128)(2,1)S(1)} all-to-all(bf16[2,2,131072]{2,1,0:T(2,128)(2,1)S(1)} %reshape.61), channel_id=1, replica_groups=mesh['hi'=4,'mid'=4,'lo'=2] {'lo'}, dimensions={0} | all-to-all | bytes 2097152 | tf_op jit(solution)/shard_map/all_to_all | solution.py:68
  111.4 0.9 reshape.62
  112.3 0.4 copy.67
  112.7 1.1 copy.65
  113.8 1.2 %reshape.58 = bf16[512,1024]{1,0:T(8,128)(2,1)} reshape(bf16[256,2,1,1024]{3,1,0,2:T(2,128)(2,1)S(1)} %copy.65) | data formatting | bytes 2097152 | tf_op jit(solution)/shard_map/reshape | solution.py:68
  (3 shorter events, 0.0 us)
Async XLA Ops:
  2.1 9.3 %copy-start = (s32[14]{0:T(128)S(1)}, s32[14]{0:T(128)}, u32[]{:S(2)}) copy-start(s32[14]{0:T(128)} %param.5) | copy-start | bytes 172
  3.7 30.3 %all-to-all-start = ((bf16[32,32,512]{2,0,1:T(8,128)(2,1)}), bf16[32,32,512]{2,0,1:T(8,128)(2,1)S(1)}, u32[]{:S(2)}, u32[]{:S(2)}) async-start(bf16[32,32,512]{2,0,1:T(8,128)(2,1)} %copy.56), calls=%async_computation | async-start | bytes 2097152 | tf_op jit(solution)/shard_map/all_to_all | solution.py:37
where the time goes:
time: 116 us; the launch traced here: 115 us
  blocking collectives  65.2 us (56%)
  local copies, waits for them, and re-layouts  15.7 us (14%)
  waiting for transfers between devices  15.5 us (13%)
  matrix products  9.51 us (8%)
  starting transfers between devices  7.39 us (6%)
  other arithmetic  1.59 us (1%)
    all_to_all x1, blocking collectives, on_device(): lax.all_to_all(mixed_pass, ('hi', 'mid'), split_axis=0, concat_axis=1, ti...  31.3 us
    all_to_all x1, blocking collectives, on_device(): lax.all_to_all(third_pass.reshape(BLOCK // lo_count, lo_count, up_cols),...  17.5 us
    all_to_all x1, blocking collectives, on_device(): lax.all_to_all(fourth_pass, 'lo', split_axis=0, concat_axis=1, tiled=True)  16.5 us
    all_to_all x1, waiting for transfers between devices, on_device(): lax.all_to_all(first_pass, ('hi', 'mid'), split_axis=1, concat_axis=0, ti...  15.5 us
    all_to_all x1, starting transfers between devices, on_device(): lax.all_to_all(first_pass, ('hi', 'mid'), split_axis=1, concat_axis=0, ti...  7.39 us
    reshape x2, local copies, waits for them, and re-layouts, on_device(): diagonal_factor(up_index, down_index, coupling_seed)  5.05 us
    unnamed x6, local copies, waits for them, and re-layouts  2.63 us
  transfers between devices with their start and end apart: 1, of which 1 were waited for; matrix products, arithmetic and copies ran while one was open for 6% of the time, Pallas kernels for 0%

commit v1 on v0

--- a/solution.py
+++ b/solution.py
@@ -65,9 +65,12 @@
     fourth_pass = jnp.einsum(
         "gh,hpu->gpu", hop_blocks[3], gathered, preferred_element_type=jnp.float32
     ).astype(jnp.bfloat16)
-    result = lax.all_to_all(fourth_pass, "lo", split_axis=0, concat_axis=1, tiled=True).reshape(
-        down_rows, up_cols
-    )
+    result = jnp.concatenate(
+        lax.all_to_all(
+            jnp.stack(jnp.split(fourth_pass, lax.axis_size("lo"), axis=0), axis=0), "lo", 0, 0
+        ),
+        axis=1,
+    ).reshape(down_rows, up_cols)
     return result
 
 

time: 116 us -> 111 us (0.957)
  local copies, waits for them, and re-layouts: 15.7 us -> 12.6 us
  other arithmetic: 1.59 us -> 0.24 us
    unnamed x6 -> x2, local copies, waits for them, and re-layouts: 2.63 us -> 0.01 us
    convert_element_type x1 -> x0, other arithmetic: 1.45 us -> none  [on_device(): fourth_pass = jnp.einsum('gh,hpu->gpu', hop_blocks[3], gathered, preferre...]
    another operation x0 -> x2, local copies, waits for them, and re-layouts: none -> 1.29 us  [the longest x1 1.22 us: on_device(): result = jnp.concatenate(lax.all_to_all(jnp.stack(jnp.split(fourth_pass,...]
  transfers between devices with their start and end apart: 1 -> 1, of which waited for: 1 -> 1; matrix products, arithmetic and copies ran while one was open for 6% -> 7% of each run, Pallas kernels for 0% -> 0%
where the time goes in v1:
time: 111 us
  blocking collectives  65.2 us (59%)
  waiting for transfers between devices  15.5 us (14%)
  local copies, waits for them, and re-layouts  12.6 us (11%)
  matrix products  9.51 us (9%)
  starting transfers between devices  7.39 us (7%)
    all_to_all x1, blocking collectives, on_device(): lax.all_to_all(mixed_pass, ('hi', 'mid'), split_axis=0, concat_axis=1, ti...  31.3 us
    all_to_all x1, blocking collectives, on_device(): lax.all_to_all(third_pass.reshape(BLOCK // lo_count, lo_count, up_cols),...  17.5 us
    all_to_all x1, blocking collectives, on_device(): lax.all_to_all(jnp.stack(jnp.split(fourth_pass, lax.axis_size('lo'), axis...  16.5 us
    all_to_all x1, waiting for transfers between devices, on_device(): lax.all_to_all(first_pass, ('hi', 'mid'), split_axis=1, concat_axis=0, ti...  15.5 us
    all_to_all x1, starting transfers between devices, on_device(): lax.all_to_all(first_pass, ('hi', 'mid'), split_axis=1, concat_axis=0, ti...  7.39 us
    reshape x2, local copies, waits for them, and re-layouts, on_device(): diagonal_factor(up_index, down_index, coupling_seed)  5.03 us
  transfers between devices with their start and end apart: 1, of which 1 were waited for; matrix products, arithmetic and copies ran while one was open for 7% of the time, Pallas kernels for 0%

profile of v1, /device:TPU:0, one launch (start us, length us, event | category | flops | bytes accessed | tf_op | source)
XLA Modules:
  0.0 110.6 jit_solution(7790981644420754204)
XLA Ops:
  0.0 2.1 %convolution_convert_fusion.2 = bf16[512,512,2]{1,0,2:T(8,128)(2,1)S(1)} fusion(bf16[64,2,8,512]{3,2,1,0:T(8,128)(2,1)} %bitcast.57, bf16[4,512,512]{2,1,0:T(8,128)(2,1)} %param.4), kind=kOutput, calls=%fused_computation.5 | convolution fusion | flops 537395200 | bytes 2621440 | tf_op jit(solution)/shard_map/dav,wv->awd/dot_general | solution.py:31
  2.1 0.0 copy-start
  2.1 1.5 %copy.33 = bf16[32,32,512]{2,0,1:T(8,128)(2,1)} copy(bf16[32,32,512]{2,1,0:T(8,128)(2,1)S(1)} %bitcast.56) | data formatting | bytes 2097152 | tf_op jit(solution)/shard_map/reshape | solution.py:36
  3.7 7.4 %all-to-all-start = ((bf16[32,32,512]{2,0,1:T(8,128)(2,1)}), bf16[32,32,512]{2,0,1:T(8,128)(2,1)S(1)}, u32[]{:S(2)}, u32[]{:S(2)}) async-start(bf16[32,32,512]{2,0,1:T(8,128)(2,1)} %copy.33), calls=%async_computation | async-start | bytes 2097152 | tf_op jit(solution)/shard_map/all_to_all | solution.py:37
  11.1 0.1 iota_add_fusion
  11.2 0.2 add.50
  11.4 0.0 copy-done
  11.5 2.0 %negate_exponential_fusion = f32[1024,512]{1,0:T(8,128)S(1)} fusion(s32[512]{0:T(512)S(1)} %iota_add_fusion.1, f32[14]{0:T(128)S(1)} %convert_multiply_fusion, s32[1024]{0:T(1024)S(1)} %add.50), kind=kOutput, calls=%fused_computation.2 | convolution fusion | flops 88683520 | bytes 2103352 | tf_op jit(solution)/shard_map/dot_general | solution.py:20
  13.4 2.3 %reshape.57 = f32[512,2,512]{2,1,0:T(2,128)} reshape(f32[1024,512]{1,0:T(8,128)S(1)} %negate_exponential_fusion) | data formatting | bytes 4194304 | tf_op jit(solution)/shard_map/reshape | solution.py:48
  15.7 2.7 %copy.36 = f32[512,2,512]{0,2,1:T(8,128)S(1)} copy(f32[512,2,512]{2,1,0:T(2,128)} %reshape.57) | data formatting | bytes 4194304 | tf_op jit(solution)/shard_map/reshape | solution.py:48
  18.5 15.5 %all-to-all-done = bf16[32,32,512]{2,0,1:T(8,128)(2,1)S(1)} async-done(((bf16[32,32,512]{2,0,1:T(8,128)(2,1)}), bf16[32,32,512]{2,0,1:T(8,128)(2,1)S(1)}, u32[]{:S(2)}, u32[]{:S(2)}) %all-to-all-start) | async-done | bytes 1048608 | tf_op jit(solution)/shard_map/all_to_all | solution.py:37
  34.0 0.1 copy.34
  34.1 1.8 %fusion = bf16[512,2,512]{0,2,1:T(8,128)(2,1)S(1)} fusion(f32[512,2,512]{0,2,1:T(8,128)S(1)} %copy.36, bf16[512,2,512]{2,0,1:T(8,128)(2,1)S(1)} %bitcast.54, bf16[4,512,512]{2,1,0:T(8,128)(2,1)} %param.4), kind=kOutput, calls=%fused_computation.1 | convolution fusion | flops 537919488 | bytes 4718592 | tf_op jit(solution)/shard_map/gh,hpd->gpd/dot_general | solution.py:38
  35.9 1.0 copy.37
  36.9 31.3 %all_to_all.53 = bf16[512,2,512]{2,1,0:T(2,128)(2,1)S(1)} all-to-all(bf16[512,2,512]{2,1,0:T(2,128)(2,1)S(1)} %copy.37), channel_id=1, replica_groups=mesh['hi'=4,'mid'=4,'lo'=2] {'hi','mid'}, dimensions={0} | all-to-all | bytes 2097152 | tf_op jit(solution)/shard_map/all_to_all | solution.py:52
  68.1 0.2 copy.38
  68.3 1.1 copy.39
  69.4 0.4 reshape.58
  69.8 1.8 %fusion.1 = bf16[512,1024]{1,0:T(8,128)(2,1)S(1)} fusion(bf16[1024,512]{1,0:T(8,128)(2,1)S(1)} %reshape.58, bf16[4,512,512]{2,1,0:T(8,128)(2,1)} %param.4), kind=kOutput, calls=%fused_computation.6 | convolution fusion | flops 537395200 | bytes 2621440 | tf_op jit(solution)/shard_map/ud,ed->eu/dot_general | solution.py:55
  71.6 0.4 reshape.59
  72.1 0.3 copy.40
  72.4 17.5 %all_to_all.54 = bf16[256,2,1024]{2,0,1:T(8,128)(2,1)S(1)} all-to-all(bf16[256,2,1024]{2,0,1:T(8,128)(2,1)S(1)} %copy.40), channel_id=1, replica_groups=mesh['hi'=4,'mid'=4,'lo'=2] {'lo'}, dimensions={1} | all-to-all | bytes 2097152 | tf_op jit(solution)/shard_map/all_to_all | solution.py:58
  89.8 1.8 %fusion.2 = bf16[512,1024]{0,1:T(8,128)(2,1)S(1)} fusion(bf16[512,1024]{1,0:T(8,128)(2,1)S(1)} %bitcast.55, bf16[4,512,512]{2,1,0:T(8,128)(2,1)} %param.4), kind=kOutput, calls=%fused_computation.7 | convolution fusion | flops 537395200 | bytes 2621440 | tf_op jit(solution)/shard_map/gh,hpu->gpu/dot_general | solution.py:65
  91.6 0.1 slice_bitcast_fusion.1
  91.7 0.1 pad_maximum_fusion
  91.8 16.5 %all_to_all.55 = bf16[2,256,1,1024]{1,3,2,0:T(8,128)(2,1)S(1)} all-to-all(bf16[2,256,1,1024]{1,3,2,0:T(8,128)(2,1)S(1)} %pad_maximum_fusion), channel_id=1, replica_groups=mesh['hi'=4,'mid'=4,'lo'=2] {'lo'}, dimensions={0} | all-to-all | bytes 2097152 | tf_op jit(solution)/shard_map/all_to_all | solution.py:69
  108.3 1.1 copy.41
  109.4 1.2 %reshape_reshape.3 = bf16[512,1024]{1,0:T(8,128)(2,1)} reshape(bf16[256,2,1,1024]{3,1,0,2:T(2,128)(2,1)S(1)} %copy.41) | data formatting | bytes 2097152 | tf_op jit(solution)/shard_map/reshape;reshape | solution.py:73
  (3 shorter events, 0.0 us)
Async XLA Ops:
  2.1 9.3 %copy-start = (s32[14]{0:T(128)S(1)}, s32[14]{0:T(128)}, u32[]{:S(2)}) copy-start(s32[14]{0:T(128)} %param.5) | copy-start | bytes 172
  3.7 30.3 %all-to-all-start = ((bf16[32,32,512]{2,0,1:T(8,128)(2,1)}), bf16[32,32,512]{2,0,1:T(8,128)(2,1)S(1)}, u32[]{:S(2)}, u32[]{:S(2)}) async-start(bf16[32,32,512]{2,0,1:T(8,128)(2,1)} %copy.33), calls=%async_computation | async-start | bytes 2097152 | tf_op jit(solution)/shard_map/all_to_all | solution.py:37
